TPU v7x, 32 devices: a whole 2x2x4 slice. The times are simulated.
32 devices in a mesh: slab: 8 (over z, y), mem: 4 (over x, core).
Axes of the slice: x: 2, y: 2, z: 4, core: 2. Of those that a mesh axis runs over, the one named last changes fastest.
Arguments:
- starting_states_set: float32 [128, 64, 1024], P('mem', 'slab'), may hold values from -6 to 6
- land_mask: int32 [64, 1024], P('slab'), may hold values 0 or 1
- cell_class: int32 [64, 1024], P('slab'), may hold values from 0 to 7
- kappa_table: float32 [8], replicated, may hold values from 0.08 to 0.2
- flow_table: float32 [2, 8], replicated, may hold values from -0.3 to 0.3
- obs_index: int32 [1024], P('slab'), may hold values from 0 to 8191
- obs_values: float32 [1024], P('slab'), may hold values from -24 to 24
- obs_var: float32 [1024], P('slab'), may hold values from 0.1 to 1
Outputs:
- analysis: float32 [128, 64, 1024], P('mem', 'slab')
All inputs are finite; a program needn't handle non-finite values. No bound on the sum of `land_mask` on one device may be relied on, other than what follows from the above.
Results may differ from a plain program's by a relative error of at most 0.00016.
Values sent between devices are 32-bit elements; how exact they have to be, the bound alone decides.
A program may use at most 64 MiB of HBM per device.

v0:
```python
import jax
import jax.numpy as jnp
from jax import lax
from jax.sharding import PartitionSpec as P

STEPS = 8
ROOT_ITERATIONS = 8
NCLS = 8


def extended(block, sides, width):
    for axis, dim in sides:
        count = lax.axis_size(axis)
        forward = [(i, i + 1) for i in range(count - 1)]
        backward = [(target, source) for source, target in forward]
        low = lax.ppermute(
            lax.slice_in_dim(block, block.shape[dim] - width, None, axis=dim), axis, forward
        )
        high = lax.ppermute(lax.slice_in_dim(block, 0, width, axis=dim), axis, backward)
        block = jnp.concatenate([low, block, high], axis=dim)
    return block


def advance(center, north, south, diffusion, flow_east, flow_north, wet_cells):
    edge = jnp.zeros_like(center[..., :1])
    east = jnp.concatenate([center[..., 1:], edge], axis=-1)
    west = jnp.concatenate([edge, center[..., :-1]], axis=-1)
    spread = north + south + east + west - 4.0 * center
    return wet_cells * (
        center
        + diffusion * spread
        - 0.5 * flow_east * (east - west)
        - 0.5 * flow_north * (north - south)
    )


def coefficients(classes, mask_rows, kappa_table, flow_table):
    diffusion = jnp.zeros(classes.shape, jnp.float32)
    flow_east = jnp.zeros(classes.shape, jnp.float32)
    flow_north = jnp.zeros(classes.shape, jnp.float32)
    for label in range(NCLS):
        hit = classes == label
        diffusion = diffusion + jnp.where(hit, kappa_table[label], 0.0)
        flow_east = flow_east + jnp.where(hit, flow_table[0, label], 0.0)
        flow_north = flow_north + jnp.where(hit, flow_table[1, label], 0.0)
    return (diffusion, flow_east, flow_north, mask_rows.astype(jnp.float32))


def statistics(observed, values, variances, factor, ens_total):
    highest = lax.Precision.HIGHEST
    ybar = jnp.sum(observed, axis=0) / ens_total
    err = variances * factor
    anom = (observed - ybar) / jnp.sqrt(err * (ens_total - 1.0))
    dev = (values - ybar) / jnp.sqrt(err)
    return (jnp.dot(anom, anom.T, precision=highest), jnp.dot(anom, dev, precision=highest))


def local(
    starting_states_set,
    land_mask,
    cell_class,
    kappa_table,
    flow_table,
    obs_index,
    obs_values,
    obs_var,
):
    highest = lax.Precision.HIGHEST
    kd = starting_states_set.shape[0]
    rows = starting_states_set.shape[1]
    ens_total = kd * lax.axis_size("mem")
    current_profile = starting_states_set
    diffusion, flow_east, flow_north, wet_cells = coefficients(
        cell_class, land_mask, kappa_table, flow_table
    )
    for step in range(STEPS):
        padded = extended(current_profile, (("slab", 1),), 1)
        current_profile = advance(
            padded[:, 1:-1],
            padded[:, 2:],
            padded[:, :-2],
            diffusion,
            flow_east,
            flow_north,
            wet_cells,
        )
    raveled_vector = current_profile.reshape(kd, rows * current_profile.shape[2])
    observed = jnp.take(raveled_vector, obs_index, axis=1)
    slab_here = lax.axis_index("slab").astype(jnp.float32)
    factor = 1.0 + 2.0 * slab_here / float(lax.axis_size("slab") - 1)
    member_group = lax.axis_index("mem")
    columns = lax.all_to_all(observed, "mem", split_axis=1, concat_axis=0, tiled=True)
    count = columns.shape[1]
    values = lax.dynamic_slice_in_dim(obs_values, member_group * count, count)
    variances = lax.dynamic_slice_in_dim(obs_var, member_group * count, count)
    gram_part, proj_part = statistics(columns, values, variances, factor, ens_total)
    gram, proj = lax.psum((gram_part, proj_part), ("slab", "mem"))
    ident = jnp.eye(ens_total, dtype=jnp.float32)
    matrix = ident + gram
    scale = jnp.trace(matrix)
    upper = matrix / scale
    lower = ident
    for turn in range(ROOT_ITERATIONS):
        factor_q = 1.5 * ident - 0.5 * jnp.dot(lower, upper, precision=highest)
        upper = jnp.dot(upper, factor_q, precision=highest)
        lower = jnp.dot(factor_q, lower, precision=highest)
    transform_weights = lower / jnp.sqrt(scale)
    mean_w = jnp.dot(lower, jnp.dot(lower, proj, precision=highest), precision=highest) / (
        scale * jnp.sqrt(ens_total - 1.0)
    )
    total_w = transform_weights + mean_w[:, None]
    omega = 1.0 / ens_total + total_w - (jnp.sum(total_w, axis=0) / ens_total)[None, :]
    mixed = jnp.einsum(
        "ij,irc->jrc",
        omega,
        lax.all_to_all(current_profile, "mem", split_axis=2, concat_axis=0, tiled=True),
        precision=highest,
    )
    return lax.all_to_all(mixed, "mem", split_axis=0, concat_axis=2, tiled=True)


def solution(mesh):
    return jax.shard_map(
        local,
        mesh=mesh,
        in_specs=(
            P("mem", "slab", None),
            P("slab", None),
            P("slab", None),
            P(),
            P(),
            P("slab"),
            P("slab"),
            P("slab"),
        ),
        out_specs=P("mem", "slab", None),
        check_vma=False,
    )
```

profile of v0, /device:TPU:0, one launch (start us, length us, event | category | flops | bytes accessed | tf_op | source)
XLA Modules:
  0.0 308.6 jit_solution(16976725727790895447)
XLA Ops:
  6.5 1.9 copy.42
  10.5 5.5 %collective-permute-start.1 = (f32[32,1,1024]{2,0,1:T(8,128)}, f32[32,1,1024]{2,0,1:T(8,128)S(1)}, u32[]{:S(2)}, u32[]{:S(2)}) collective-permute-start(f32[32,1,1024]{2,0,1:T(8,128)} %get-tuple-element.42), channel_id=1, source_target_pairs={{0,4},{4,8},{8,12},{12,16},{16,20},{20,24},{24,28},{1,5},{5,9},{9,... | collective-permute-start | bytes 393224 | tf_op jit(solution)/shard_map/ppermute | solution.py:16
  17.8 5.0 %select_add_fusion = (f32[8,1024]{1,0:T(8,128)S(1)}, pred[8,1024]{1,0:T(8,128)(4,1)S(1)}, pred[8,1024]{1,0:T(8,128)(4,1)S(1)}, pred[8,1024]{1,0:T(8,128)(4,1)S(1...) fusion(f32[]{:T(128)} %bitcast.7, f32[]{:T(128)} %bitcast.6, ...), kind=kLoop, calls=%fused_computation.61 | loop fusion | flops 188416 | bytes 131104 | tf_op jit(solution)/shard_map/add | solution.py:43
  22.8 5.0 %add_multiply_fusion = f32[8,1024]{1,0:T(8,128)S(1)} fusion(pred[8,1024]{1,0:T(8,128)(4,1)S(1)} %get-tuple-element.13, pred[8,1024]{1,0:T(8,128)(4,1)S(1)} %get-tuple-element.12, pred[8,1024]{1,0:T(8,128)(4,1)S(1)} %get-tuple-element.11, pred[8,1024]{1,0:T(8,128)(4,1)S(1)} %get-tuple-element.10, pred[8,1024]{1,0:T(8,128)(4,1)S(1)} %get-tuple-element.9, ...), kind=kLoop, calls=%fused_computation.59 | loop fusion | flops 131072 | bytes 98336 | tf_op jit(solution)/shard_map/mul | solution.py:33
  27.8 5.0 %add_multiply_fusion.1 = f32[8,1024]{1,0:T(8,128)S(1)} fusion(pred[8,1024]{1,0:T(8,128)(4,1)S(1)} %get-tuple-element.13, pred[8,1024]{1,0:T(8,128)(4,1)S(1)} %get-tuple-element.12, pred[8,1024]{1,0:T(8,128)(4,1)S(1)} %get-tuple-element.11, pred[8,1024]{1,0:T(8,128)(4,1)S(1)} %get-tuple-element.10, pred[8,1024]{1,0:T(8,128)(4,1)S(1)} %get-tuple-element.9, ...), kind=kLoop, calls=%fused_computation.60 | loop fusion | flops 131072 | bytes 98336 | tf_op jit(solution)/shard_map/mul | solution.py:32
  35.0 5.4 %collective-permute-start.3 = (f32[32,1,1024]{2,0,1:T(8,128)S(1)}, f32[32,1,1024]{2,0,1:T(8,128)S(1)}, u32[]{:S(2)}, u32[]{:S(2)}) collective-permute-start(f32[32,1,1024]{2,0,1:T(8,128)S(1)} %get-tuple-element.38), channel_id=1, source_target_pairs={{0,4},{4,8},{8,12},{12,16},{16,20},{20,24},{24,28},{1,5},{5,9},{9,... | collective-permute-start | bytes 393224 | tf_op jit(solution)/shard_map/ppermute | solution.py:16
  41.4 2.9 collective-permute-done.3
  46.4 5.0 %collective-permute-start.5 = (f32[32,1,1024]{2,0,1:T(8,128)S(1)}, f32[32,1,1024]{2,0,1:T(8,128)S(1)}, u32[]{:S(2)}, u32[]{:S(2)}) collective-permute-start(f32[32,1,1024]{2,0,1:T(8,128)S(1)} %get-tuple-element.34), channel_id=1, source_target_pairs={{0,4},{4,8},{8,12},{12,16},{16,20},{20,24},{24,28},{1,5},{5,9},{9,... | collective-permute-start | bytes 393224 | tf_op jit(solution)/shard_map/ppermute | solution.py:16
  52.9 3.0 collective-permute-done.5
  57.8 5.0 %collective-permute-start.7 = (f32[32,1,1024]{2,0,1:T(8,128)S(1)}, f32[32,1,1024]{2,0,1:T(8,128)S(1)}, u32[]{:S(2)}, u32[]{:S(2)}) collective-permute-start(f32[32,1,1024]{2,0,1:T(8,128)S(1)} %get-tuple-element.30), channel_id=1, source_target_pairs={{0,4},{4,8},{8,12},{12,16},{16,20},{20,24},{24,28},{1,5},{5,9},{9,... | collective-permute-start | bytes 393224 | tf_op jit(solution)/shard_map/ppermute | solution.py:16
  64.6 3.0 collective-permute-done.7
  69.5 5.0 %collective-permute-start.9 = (f32[32,1,1024]{2,0,1:T(8,128)S(1)}, f32[32,1,1024]{2,0,1:T(8,128)S(1)}, u32[]{:S(2)}, u32[]{:S(2)}) collective-permute-start(f32[32,1,1024]{2,0,1:T(8,128)S(1)} %get-tuple-element.26), channel_id=1, source_target_pairs={{0,4},{4,8},{8,12},{12,16},{16,20},{20,24},{24,28},{1,5},{5,9},{9,... | collective-permute-start | bytes 393224 | tf_op jit(solution)/shard_map/ppermute | solution.py:16
  76.3 3.0 collective-permute-done.9
  81.3 5.0 %collective-permute-start.11 = (f32[32,1,1024]{2,0,1:T(8,128)S(1)}, f32[32,1,1024]{2,0,1:T(8,128)S(1)}, u32[]{:S(2)}, u32[]{:S(2)}) collective-permute-start(f32[32,1,1024]{2,0,1:T(8,128)S(1)} %get-tuple-element.22), channel_id=1, source_target_pairs={{0,4},{4,8},{8,12},{12,16},{16,20},{20,24},{24,28},{1,5},{5,9},{9,... | collective-permute-start | bytes 393224 | tf_op jit(solution)/shard_map/ppermute | solution.py:16
  88.0 3.0 collective-permute-done.11
  93.0 5.0 %collective-permute-start.13 = (f32[32,1,1024]{2,0,1:T(8,128)S(1)}, f32[32,1,1024]{2,0,1:T(8,128)S(1)}, u32[]{:S(2)}, u32[]{:S(2)}) collective-permute-start(f32[32,1,1024]{2,0,1:T(8,128)S(1)} %get-tuple-element.18), channel_id=1, source_target_pairs={{0,4},{4,8},{8,12},{12,16},{16,20},{20,24},{24,28},{1,5},{5,9},{9,... | collective-permute-start | bytes 393224 | tf_op jit(solution)/shard_map/ppermute | solution.py:16
  99.7 3.0 collective-permute-done.13
  104.7 5.0 %collective-permute-start.15 = (f32[32,1,1024]{2,0,1:T(8,128)S(1)}, f32[32,1,1024]{2,0,1:T(8,128)S(1)}, u32[]{:S(2)}, u32[]{:S(2)}) collective-permute-start(f32[32,1,1024]{2,0,1:T(8,128)S(1)} %get-tuple-element.14), channel_id=1, source_target_pairs={{0,4},{4,8},{8,12},{12,16},{16,20},{20,24},{24,28},{1,5},{5,9},{9,... | collective-permute-start | bytes 393224 | tf_op jit(solution)/shard_map/ppermute | solution.py:16
  111.5 3.0 collective-permute-done.15
  115.1 2.6 copy.43
  117.7 2.8 gather_fusion
  121.4 3.4 %all-to-all-start = ((f32[4,1,1024]{2,1,0:T(1,128)}), f32[4,1,1024]{2,1,0:T(1,128)S(1)}, u32[]{:S(2)}, u32[]{:S(2)}) async-start(f32[4,1,1024]{2,1,0:T(1,128)} %reshape.69), calls=%async_computation | async-start | bytes 32768 | tf_op jit(solution)/shard_map/all_to_all | solution.py:92
  124.9 2.7 copy.46
  127.6 4.8 %reshape.67 = f32[4,1,65536]{2,1,0:T(1,128)} reshape(f32[1024,8,32]{2,1,0:T(8,128)} %bitcast.117) | data formatting | bytes 2097152
  132.4 3.5 %all-to-all-start.1 = ((f32[4,1,65536]{2,1,0:T(1,128)}), f32[4,1,65536]{2,1,0:T(1,128)S(1)}, u32[]{:S(2)}, u32[]{:S(2)}) async-start(f32[4,1,65536]{2,1,0:T(1,128)} %reshape.67), calls=%async_computation.1 | async-start | bytes 2097152 | tf_op jit(solution)/shard_map/all_to_all | solution.py:116
  139.1 44.7 %psum.15 = f32[128]{0:T(128)S(1)} all-reduce(f32[128]{0:T(128)S(1)} %convolution_bitcast_fusion.2), channel_id=1, replica_groups=mesh['slab'=8,'mem'=4] {'slab','mem'}, use_global_device_ids=true, to_apply=%region_3.4 | all-reduce | flops 128 | bytes 1024 | tf_op jit(solution)/shard_map/psum | solution.py:97
  183.8 76.2 %all-reduce.18.cloned.1.call-done = f32[128,128]{1,0:T(8,128)} async-done(((f32[128,128]{1,0:T(8,128)}), f32[128,128]{1,0:T(8,128)}) %all-reduce.18.cloned.1.call-update) | async-done | bytes 65552 | tf_op jit(solution)/shard_map/psum | solution.py:97
  263.2 1.6 fusion.17
  270.8 3.7 %reduce.2 = f32[4,65536]{1,0:T(4,128)S(1)} reduce(f32[4,1,65536]{2,1,0:T(1,128)S(1)} %all-to-all-done.1, f32[]{:T(128)} %broadcast.130), dimensions={1}, to_apply=%all_to_all.41.reduce_sub_computation | reduce | bytes 2097156 | tf_op jit(solution)/shard_map/all_to_all | solution.py:116
  274.5 3.4 %reshape.68 = f32[1024,8,32]{2,1,0:T(8,128)} reshape(f32[4,65536]{1,0:T(4,128)S(1)} %reduce.2) | data formatting | bytes 2097152
  277.9 2.8 copy.47
  282.4 18.2 %all_to_all.52 = f32[128,8,256]{2,1,0:T(8,128)S(1)} all-to-all(f32[128,8,256]{2,1,0:T(8,128)S(1)} %copy.49), channel_id=1, replica_groups=mesh['slab'=8,'mem'=4] {'mem'}, dimensions={0} | all-to-all | bytes 2097152 | tf_op jit(solution)/shard_map/all_to_all | solution.py:119
  (112 shorter events, 44.0 us)
Async XLA Ops:
  6.5 9.8 %copy-start.2 = (f32[8]{0:T(128)S(1)}, f32[8]{0:T(128)}, u32[]{:S(2)}) copy-start(f32[8]{0:T(128)} %param.11) | copy-start | bytes 100
  6.5 10.5 %copy-start = (f32[2,8]{1,0:T(2,128)S(1)}, f32[2,8]{1,0:T(2,128)}, u32[]{:S(2)}) copy-start(f32[2,8]{1,0:T(2,128)} %param.12) | copy-start | bytes 196
  6.5 11.2 %copy-start.5 = (s32[128]{0:T(128)S(1)}, s32[128]{0:T(128)}, u32[]{:S(2)}) copy-start(s32[128]{0:T(128)} %param.13) | copy-start | bytes 1540
  6.5 11.2 %copy-start.3 = (s32[8,1024]{1,0:T(8,128)S(1)}, s32[8,1024]{1,0:T(8,128)}, u32[]{:S(2)}) copy-start(s32[8,1024]{1,0:T(8,128)} %param.10) | copy-start | bytes 98308
  6.5 26.3 %copy-start.1 = (s32[8,1024]{1,0:T(8,128)S(1)}, s32[8,1024]{1,0:T(8,128)}, u32[]{:S(2)}) copy-start(s32[8,1024]{1,0:T(8,128)} %param.9) | copy-start | bytes 98308
  9.2 23.8 %collective-permute-start = (f32[32,1,1024]{2,0,1:T(8,128)}, f32[32,1,1024]{2,0,1:T(8,128)S(1)}, u32[]{:S(2)}, u32[]{:S(2)}) collective-permute-start(f32[32,1,1024]{2,0,1:T(8,128)} %get-tuple-element.43), channel_id=1, source_target_pairs={{4,0},{8,4},{12,8},{16,12},{20,16},{24,20},{28,24},{5,1},{9,5},{13... | collective-permute-start | bytes 393224 | tf_op jit(solution)/shard_map/ppermute | solution.py:19
  10.5 22.5 %collective-permute-start.1 = (f32[32,1,1024]{2,0,1:T(8,128)}, f32[32,1,1024]{2,0,1:T(8,128)S(1)}, u32[]{:S(2)}, u32[]{:S(2)}) collective-permute-start(f32[32,1,1024]{2,0,1:T(8,128)} %get-tuple-element.42), channel_id=1, source_target_pairs={{0,4},{4,8},{8,12},{12,16},{16,20},{20,24},{24,28},{1,5},{5,9},{9,... | collective-permute-start | bytes 393224 | tf_op jit(solution)/shard_map/ppermute | solution.py:16
  33.7 7.8 %collective-permute-start.2 = (f32[32,1,1024]{2,0,1:T(8,128)S(1)}, f32[32,1,1024]{2,0,1:T(8,128)S(1)}, u32[]{:S(2)}, u32[]{:S(2)}) collective-permute-start(f32[32,1,1024]{2,0,1:T(8,128)S(1)} %get-tuple-element.39), channel_id=1, source_target_pairs={{4,0},{8,4},{12,8},{16,12},{20,16},{24,20},{28,24},{5,1},{9,5},{13... | collective-permute-start | bytes 393224 | tf_op jit(solution)/shard_map/ppermute | solution.py:19
  35.0 9.4 %collective-permute-start.3 = (f32[32,1,1024]{2,0,1:T(8,128)S(1)}, f32[32,1,1024]{2,0,1:T(8,128)S(1)}, u32[]{:S(2)}, u32[]{:S(2)}) collective-permute-start(f32[32,1,1024]{2,0,1:T(8,128)S(1)} %get-tuple-element.38), channel_id=1, source_target_pairs={{0,4},{4,8},{8,12},{12,16},{16,20},{20,24},{24,28},{1,5},{5,9},{9,... | collective-permute-start | bytes 393224 | tf_op jit(solution)/shard_map/ppermute | solution.py:16
  45.1 7.8 %collective-permute-start.4 = (f32[32,1,1024]{2,0,1:T(8,128)S(1)}, f32[32,1,1024]{2,0,1:T(8,128)S(1)}, u32[]{:S(2)}, u32[]{:S(2)}) collective-permute-start(f32[32,1,1024]{2,0,1:T(8,128)S(1)} %get-tuple-element.35), channel_id=1, source_target_pairs={{4,0},{8,4},{12,8},{16,12},{20,16},{24,20},{28,24},{5,1},{9,5},{13... | collective-permute-start | bytes 393224 | tf_op jit(solution)/shard_map/ppermute | solution.py:19
  46.4 9.5 %collective-permute-start.5 = (f32[32,1,1024]{2,0,1:T(8,128)S(1)}, f32[32,1,1024]{2,0,1:T(8,128)S(1)}, u32[]{:S(2)}, u32[]{:S(2)}) collective-permute-start(f32[32,1,1024]{2,0,1:T(8,128)S(1)} %get-tuple-element.34), channel_id=1, source_target_pairs={{0,4},{4,8},{8,12},{12,16},{16,20},{20,24},{24,28},{1,5},{5,9},{9,... | collective-permute-start | bytes 393224 | tf_op jit(solution)/shard_map/ppermute | solution.py:16
  56.5 8.1 %collective-permute-start.6 = (f32[32,1,1024]{2,0,1:T(8,128)S(1)}, f32[32,1,1024]{2,0,1:T(8,128)S(1)}, u32[]{:S(2)}, u32[]{:S(2)}) collective-permute-start(f32[32,1,1024]{2,0,1:T(8,128)S(1)} %get-tuple-element.31), channel_id=1, source_target_pairs={{4,0},{8,4},{12,8},{16,12},{20,16},{24,20},{28,24},{5,1},{9,5},{13... | collective-permute-start | bytes 393224 | tf_op jit(solution)/shard_map/ppermute | solution.py:19
  57.8 9.7 %collective-permute-start.7 = (f32[32,1,1024]{2,0,1:T(8,128)S(1)}, f32[32,1,1024]{2,0,1:T(8,128)S(1)}, u32[]{:S(2)}, u32[]{:S(2)}) collective-permute-start(f32[32,1,1024]{2,0,1:T(8,128)S(1)} %get-tuple-element.30), channel_id=1, source_target_pairs={{0,4},{4,8},{8,12},{12,16},{16,20},{20,24},{24,28},{1,5},{5,9},{9,... | collective-permute-start | bytes 393224 | tf_op jit(solution)/shard_map/ppermute | solution.py:16
  68.2 8.1 %collective-permute-start.8 = (f32[32,1,1024]{2,0,1:T(8,128)S(1)}, f32[32,1,1024]{2,0,1:T(8,128)S(1)}, u32[]{:S(2)}, u32[]{:S(2)}) collective-permute-start(f32[32,1,1024]{2,0,1:T(8,128)S(1)} %get-tuple-element.27), channel_id=1, source_target_pairs={{4,0},{8,4},{12,8},{16,12},{20,16},{24,20},{28,24},{5,1},{9,5},{13... | collective-permute-start | bytes 393224 | tf_op jit(solution)/shard_map/ppermute | solution.py:19
  69.5 9.7 %collective-permute-start.9 = (f32[32,1,1024]{2,0,1:T(8,128)S(1)}, f32[32,1,1024]{2,0,1:T(8,128)S(1)}, u32[]{:S(2)}, u32[]{:S(2)}) collective-permute-start(f32[32,1,1024]{2,0,1:T(8,128)S(1)} %get-tuple-element.26), channel_id=1, source_target_pairs={{0,4},{4,8},{8,12},{12,16},{16,20},{20,24},{24,28},{1,5},{5,9},{9,... | collective-permute-start | bytes 393224 | tf_op jit(solution)/shard_map/ppermute | solution.py:16
  80.0 8.1 %collective-permute-start.10 = (f32[32,1,1024]{2,0,1:T(8,128)S(1)}, f32[32,1,1024]{2,0,1:T(8,128)S(1)}, u32[]{:S(2)}, u32[]{:S(2)}) collective-permute-start(f32[32,1,1024]{2,0,1:T(8,128)S(1)} %get-tuple-element.23), channel_id=1, source_target_pairs={{4,0},{8,4},{12,8},{16,12},{20,16},{24,20},{28,24},{5,1},{9,5},{13... | collective-permute-start | bytes 393224 | tf_op jit(solution)/shard_map/ppermute | solution.py:19
  81.3 9.7 %collective-permute-start.11 = (f32[32,1,1024]{2,0,1:T(8,128)S(1)}, f32[32,1,1024]{2,0,1:T(8,128)S(1)}, u32[]{:S(2)}, u32[]{:S(2)}) collective-permute-start(f32[32,1,1024]{2,0,1:T(8,128)S(1)} %get-tuple-element.22), channel_id=1, source_target_pairs={{0,4},{4,8},{8,12},{12,16},{16,20},{20,24},{24,28},{1,5},{5,9},{9,... | collective-permute-start | bytes 393224 | tf_op jit(solution)/shard_map/ppermute | solution.py:16
  91.7 8.1 %collective-permute-start.12 = (f32[32,1,1024]{2,0,1:T(8,128)S(1)}, f32[32,1,1024]{2,0,1:T(8,128)S(1)}, u32[]{:S(2)}, u32[]{:S(2)}) collective-permute-start(f32[32,1,1024]{2,0,1:T(8,128)S(1)} %get-tuple-element.19), channel_id=1, source_target_pairs={{4,0},{8,4},{12,8},{16,12},{20,16},{24,20},{28,24},{5,1},{9,5},{13... | collective-permute-start | bytes 393224 | tf_op jit(solution)/shard_map/ppermute | solution.py:19
  93.0 9.7 %collective-permute-start.13 = (f32[32,1,1024]{2,0,1:T(8,128)S(1)}, f32[32,1,1024]{2,0,1:T(8,128)S(1)}, u32[]{:S(2)}, u32[]{:S(2)}) collective-permute-start(f32[32,1,1024]{2,0,1:T(8,128)S(1)} %get-tuple-element.18), channel_id=1, source_target_pairs={{0,4},{4,8},{8,12},{12,16},{16,20},{20,24},{24,28},{1,5},{5,9},{9,... | collective-permute-start | bytes 393224 | tf_op jit(solution)/shard_map/ppermute | solution.py:16
  103.4 8.1 %collective-permute-start.14 = (f32[32,1,1024]{2,0,1:T(8,128)S(1)}, f32[32,1,1024]{2,0,1:T(8,128)S(1)}, u32[]{:S(2)}, u32[]{:S(2)}) collective-permute-start(f32[32,1,1024]{2,0,1:T(8,128)S(1)} %get-tuple-element.15), channel_id=1, source_target_pairs={{4,0},{8,4},{12,8},{16,12},{20,16},{24,20},{28,24},{5,1},{9,5},{13... | collective-permute-start | bytes 393224 | tf_op jit(solution)/shard_map/ppermute | solution.py:19
  104.7 9.7 %collective-permute-start.15 = (f32[32,1,1024]{2,0,1:T(8,128)S(1)}, f32[32,1,1024]{2,0,1:T(8,128)S(1)}, u32[]{:S(2)}, u32[]{:S(2)}) collective-permute-start(f32[32,1,1024]{2,0,1:T(8,128)S(1)} %get-tuple-element.14), channel_id=1, source_target_pairs={{0,4},{4,8},{8,12},{12,16},{16,20},{20,24},{24,28},{1,5},{5,9},{9,... | collective-permute-start | bytes 393224 | tf_op jit(solution)/shard_map/ppermute | solution.py:16
  114.4 10.4 %copy-start.4 = (f32[128]{0:T(128)S(1)}, f32[128]{0:T(128)}, u32[]{:S(2)}) copy-start(f32[128]{0:T(128)} %param.15) | copy-start | bytes 1540
  121.4 11.1 %all-to-all-start = ((f32[4,1,1024]{2,1,0:T(1,128)}), f32[4,1,1024]{2,1,0:T(1,128)S(1)}, u32[]{:S(2)}, u32[]{:S(2)}) async-start(f32[4,1,1024]{2,1,0:T(1,128)} %reshape.69), calls=%async_computation | async-start | bytes 32768 | tf_op jit(solution)/shard_map/all_to_all | solution.py:92
  127.6 11.3 %copy-start.6 = (f32[128]{0:T(128)S(1)}, f32[128]{0:T(128)}, u32[]{:S(2)}) copy-start(f32[128]{0:T(128)} %param.14) | copy-start | bytes 1540
  132.4 138.3 %all-to-all-start.1 = ((f32[4,1,65536]{2,1,0:T(1,128)}), f32[4,1,65536]{2,1,0:T(1,128)S(1)}, u32[]{:S(2)}, u32[]{:S(2)}) async-start(f32[4,1,65536]{2,1,0:T(1,128)} %reshape.67), calls=%async_computation.1 | async-start | bytes 2097152 | tf_op jit(solution)/shard_map/all_to_all | solution.py:116
  136.0 124.0 %all-reduce.18.cloned.1.call-start = ((), (), s32[]{:S(2)}) async-start(), calls=%async_computation.3 | async-start | bytes 131072 | tf_op jit(solution)/shard_map/psum | solution.py:97
Sparse Core Ops, SparseCore 0:
  142.4 117.4 all-reduce.17
where the time goes:
time: 310 us; the launch traced here: 309 us
  waiting for transfers between devices  105 us (34%)
  blocking collectives  62.9 us (20%)
  starting transfers between devices  58.4 us (19%)
  local copies, waits for them, and re-layouts  29.9 us (10%)
  other arithmetic  26.7 us (9%)
  between operations  15.3 us (5%)
  matrix products  10.1 us (3%)
    psum x1, waiting for transfers between devices, local(): gram, proj = lax.psum((gram_part, proj_part), ('slab', 'mem'))  76.2 us
    psum x1, blocking collectives, local(): gram, proj = lax.psum((gram_part, proj_part), ('slab', 'mem'))  44.7 us
    ppermute x8, starting transfers between devices, extended(): lax.ppermute(lax.slice_in_dim(block, block.shape[dim] - width, None, axis...  41.1 us
    ppermute x8, waiting for transfers between devices, extended(): lax.ppermute(lax.slice_in_dim(block, block.shape[dim] - width, None, axis...  20.7 us
    all_to_all x1, blocking collectives, local(): return lax.all_to_all(mixed, 'mem', split_axis=0, concat_axis=2, tiled=True)  18.2 us
    unnamed x19, local copies, waits for them, and re-layouts  10.9 us
    ppermute x8, starting transfers between devices, extended(): lax.ppermute(lax.slice_in_dim(block, 0, width, axis=dim), axis, backward)  10.3 us
    ppermute x8, waiting for transfers between devices, extended(): lax.ppermute(lax.slice_in_dim(block, 0, width, axis=dim), axis, backward)  8.4 us
  transfers between devices with their start and end apart: 19, of which 15 were waited for; matrix products, arithmetic and copies ran while one was open for 13% of the time, Pallas kernels for 0%

commit v1 on v0

v1 whole, which is shorter than its diff:
```python
import functools

import jax
import jax.numpy as jnp
from jax import lax
from jax.experimental import pallas as pl
from jax.experimental.pallas import tpu as pltpu
from jax.sharding import PartitionSpec as P

STEPS = 8
ROOT_ITERATIONS = 8
NCLS = 8
CHUNKS = 4


def halves(x):
    high = x.astype(jnp.bfloat16)
    return high, (x - high.astype(jnp.float32)).astype(jnp.bfloat16)


def left_parts(x):
    high, low = halves(x)
    return jnp.concatenate([high, high, low], axis=1)


def right_parts(x):
    high, low = halves(x)
    return jnp.concatenate([high, low, high], axis=0)


def product(left, right):
    return jnp.dot(left, right, preferred_element_type=jnp.float32)


def dot(a, b):
    return product(left_parts(a), right_parts(b))


def cycle_kernel(
    n_slab, n_mem,
    states, geo, kappa, flow, obs_index, obs_values, obs_var,
    out,
    buf, coef, geos, fore, mixed, gpart, grecv, gsum, precv, gfull,
    geo_send, geo_recv, y_send, y_recv, d_send, r_send, z_recv, keep_sem,
    a_send, a_recv, s_send, s_recv, p_send, p_recv, g_send, g_recv, b_send, b_recv,
):
    s = lax.axis_index("slab")
    m = lax.axis_index("mem")
    q, y = lax.div(s, 2), lax.rem(s, 2)
    n_pair, n_group = n_slab // 2, 2 * n_mem
    octs, rows, _, lon = states.shape[0] // 2, states.shape[1], states.shape[2], states.shape[3]
    span = lon // n_mem
    ens = fore.shape[1]
    block = ens // n_group
    kd = octs * 16
    group = y * n_mem + m
    last = n_pair - 1
    step_pair = 2 * y - 1

    def device(pair, side, member):
        return (2 * pair + side, member)

    def remote(src, dst, send, recv, where):
        return pltpu.make_async_remote_copy(
            src_ref=src, dst_ref=dst, send_sem=send, recv_sem=recv,
            device_id=where, device_id_type=pl.DeviceIdType.MESH,
        )

    def peer(k):
        other = lax.rem(group + k, n_group)
        return other, lax.div(other, n_mem), lax.rem(other, n_mem)

    barrier = pltpu.get_barrier_semaphore()
    for k in range(1, n_group):
        _, ty, tm = peer(k)
        pl.semaphore_signal(barrier, inc=1, device_id=device(q, ty, tm), device_id_type=pl.DeviceIdType.MESH)
    for k in range(1, n_pair):
        tq = lax.rem(q + k, n_pair)
        for side in range(2):
            pl.semaphore_signal(barrier, inc=1, device_id=device(tq, side, m), device_id_type=pl.DeviceIdType.MESH)
    pl.semaphore_wait(barrier, n_group - 1 + 2 * (n_pair - 1))

    def y_copy(c):
        return remote(
            states.at[octs * (1 - y) + c], buf.at[0, c, pl.ds(8 + 8 * y, 8)],
            y_send.at[c], y_recv.at[c], device(q, 1 - y, m),
        )

    def y_wait(c):
        return remote(
            states.at[c], buf.at[0, c, pl.ds(16 - 8 * y, 8)],
            y_send.at[c], y_recv.at[c], device(q, 1 - y, m),
        )

    def direct_copy(c):
        return remote(
            states.at[octs * y + c], buf.at[0, c, pl.ds(24 * (1 - y), 8)],
            d_send.at[c], z_recv.at[1 - y, c], device(q + step_pair, y, m),
        )

    def relay_copy(c):
        return remote(
            buf.at[0, c, pl.ds(16 - 8 * y, 8)], buf.at[0, c, pl.ds(24 * y, 8)],
            r_send.at[c], z_recv.at[y, c], device(q - step_pair, y, m),
        )

    def z_wait(side, c):
        return remote(
            states.at[c], buf.at[0, c, pl.ds(24 * side, 8)],
            d_send.at[c], z_recv.at[side, c], device(q, 1 - y, m),
        )

    def geo_pair():
        return remote(geo, geos.at[1 + y], geo_send.at[0], geo_recv.at[1 + y], device(q, 1 - y, m))

    def geo_side(side):
        return remote(
            geo, geos.at[3 * (1 - y)], geo_send.at[1 + side], geo_recv.at[3 * (1 - y)],
            device(q + step_pair, side, m),
        )

    def geo_wait(slot):
        return remote(geo, geos.at[slot], geo_send.at[0], geo_recv.at[slot], device(q, 1 - y, m))

    def keep(c):
        return pltpu.make_async_copy(states.at[octs * y + c], buf.at[0, c, pl.ds(8 + 8 * y, 8)], keep_sem.at[c])

    forward_edge = (q + step_pair >= 0) & (q + step_pair <= last)
    backward_edge = (q - step_pair >= 0) & (q - step_pair <= last)

    geo_pair().start()
    for c in range(octs):
        y_copy(c).start()

    @pl.when(forward_edge)
    def _():
        for side in range(2):
            geo_side(side).start()
        for c in range(octs):
            direct_copy(c).start()

    for c in range(octs):
        keep(c).start()
    geos[1 + y] = geo[...]

    @pl.when(q == 0)
    def _():
        geos[0] = jnp.zeros(geos.shape[1:], jnp.int32)
        for c in range(octs):
            buf[0, c, 0:8] = jnp.zeros((8, 8, lon), jnp.float32)

    @pl.when(q == last)
    def _():
        geos[3] = jnp.zeros(geos.shape[1:], jnp.int32)
        for c in range(octs):
            buf[0, c, 24:32] = jnp.zeros((8, 8, lon), jnp.float32)

    for c in range(octs):
        y_wait(c).wait_recv()

        @pl.when(backward_edge)
        def _():
            relay_copy(c).start()

    geo_wait(2 - y).wait_recv()

    @pl.when(q > 0)
    def _():
        geo_wait(0).wait_recv()

    @pl.when(q < last)
    def _():
        geo_wait(3).wait_recv()

    lane = lax.broadcasted_iota(jnp.int32, (8, lon), 1)

    def coefficients(k, carry):
        classes = geos[k, 0]
        wet = geos[k, 1].astype(jnp.float32)
        diffusion = jnp.zeros(classes.shape, jnp.float32)
        east = jnp.zeros(classes.shape, jnp.float32)
        north = jnp.zeros(classes.shape, jnp.float32)
        for label in range(NCLS):
            hit = classes == label
            diffusion = jnp.where(hit, kappa[label], diffusion)
            east = jnp.where(hit, flow[0, label], east)
            north = jnp.where(hit, flow[1, label], north)
        terms = (
            wet * (1.0 - 4.0 * diffusion),
            wet * (diffusion - 0.5 * north),
            wet * (diffusion + 0.5 * north),
            jnp.where(lane == lon - 1, 0.0, wet * (diffusion - 0.5 * east)),
            jnp.where(lane == 0, 0.0, wet * (diffusion + 0.5 * east)),
        )
        for index, term in enumerate(terms):
            for row in range(8):
                coef[8 * k + row, index] = jnp.broadcast_to(term[row : row + 1], (8, lon))
        return carry

    lax.fori_loop(0, 4, coefficients, 0)

    def a_copy(c, other, ty, tm):
        return remote(
            buf.at[0, c, pl.ds(8 + 8 * ty, 8), :, pl.ds(pl.multiple_of(span * tm, 128), span)],
            fore.at[:, pl.ds(pl.multiple_of(kd * m + 8 * octs * y + 8 * c, 8), 8), :],
            a_send.at[other, c], a_recv.at[group, c], device(q, ty, tm),
        )

    def a_wait(c, other, ty, tm):
        return remote(
            buf.at[0, c, pl.ds(8, 8), :, pl.ds(0, span)],
            fore.at[:, pl.ds(pl.multiple_of(kd * tm + 8 * octs * ty + 8 * c, 8), 8), :],
            a_send.at[other, c], a_recv.at[other, c], device(q, ty, tm),
        )

    def a_keep(c):
        return pltpu.make_async_copy(
            buf.at[0, c, pl.ds(8 + 8 * y, 8), :, pl.ds(pl.multiple_of(span * m, 128), span)],
            fore.at[:, pl.ds(pl.multiple_of(kd * m + 8 * octs * y + 8 * c, 8), 8), :],
            a_send.at[group, c],
        )

    for c in range(octs):
        keep(c).wait()

        @pl.when(q > 0)
        def _():
            z_wait(0, c).wait_recv()

        @pl.when(q < last)
        def _():
            z_wait(1, c).wait_recv()

        @pl.when(backward_edge)
        def _():
            relay_copy(c).wait_send()

        def two_steps(pair_step, carry):
            for parity in range(2):
                t = 2 * pair_step + parity

                def advance(r, inner):
                    center = buf[parity, c, r]
                    east = pltpu.roll(center, lon - 1, 1)
                    west = pltpu.roll(center, 1, 1)
                    buf[1 - parity, c, r] = (
                        coef[r, 0] * center
                        + coef[r, 1] * buf[parity, c, r + 1]
                        + coef[r, 2] * buf[parity, c, r - 1]
                        + coef[r, 3] * east
                        + coef[r, 4] * west
                    )
                    return inner

                lax.fori_loop(t + 1, 31 - t, advance, 0)
            return carry

        lax.fori_loop(0, STEPS // 2, two_steps, 0)
        for k in range(1, n_group):
            a_copy(c, *peer(k)).start()
        a_keep(c).start()

    for c in range(octs):
        a_keep(c).wait()
        for k in range(1, n_group):
            a_wait(c, *peer(k)).wait_recv()

    place = obs_index[...]
    n_obs = place.shape[1]
    hx = jnp.zeros((ens, n_obs), jnp.float32)
    inner = lax.broadcasted_iota(jnp.int32, (span, n_obs), 0) + span * m
    for row in range(rows):
        pick = jnp.where(inner + row * lon == place, 1.0, 0.0).astype(jnp.bfloat16)
        rest = fore[row]
        for _ in range(3):
            part = rest.astype(jnp.bfloat16)
            hx = hx + jnp.dot(part, pick, preferred_element_type=jnp.float32)
            rest = rest - part.astype(jnp.float32)
    column = place & (lon - 1)
    mine = (column >= span * m) & (column < span * m + span)
    ybar = jnp.sum(hx, axis=0, keepdims=True) / ens
    err = obs_var[...] * (1.0 + 2.0 * s.astype(jnp.float32) / float(n_slab - 1))
    anom = jnp.where(mine, (hx - ybar) / jnp.sqrt(err * (ens - 1.0)), 0.0)
    dev = (obs_values[...] - ybar) / jnp.sqrt(err)
    both = jnp.concatenate([anom, jnp.broadcast_to(dev, (ens, n_obs))], axis=0)
    high, low = halves(both)
    gpart[...] = lax.dot_general(
        left_parts(anom), jnp.concatenate([high, low, high], axis=1), (((1,), (1,)), ((), ())),
        preferred_element_type=jnp.float32,
    )

    def s_copy(other, ty, tm):
        return remote(
            gpart.at[pl.ds(pl.multiple_of(block * other, 8), block)], grecv.at[group],
            s_send.at[other], s_recv.at[group], device(q, ty, tm),
        )

    def s_wait(other, ty, tm):
        return remote(
            gpart.at[pl.ds(0, block)], grecv.at[other],
            s_send.at[other], s_recv.at[other], device(q, ty, tm),
        )

    for k in range(1, n_group):
        s_copy(*peer(k)).start()
    grecv[group] = gpart[pl.ds(pl.multiple_of(block * group, 8), block)]
    for k in range(1, n_group):
        s_wait(*peer(k)).wait_recv()
    total = grecv[0]
    for k in range(1, n_group):
        total = total + grecv[k]
    gsum[...] = total

    def p_copy(k):
        tq = lax.rem(q + k, n_pair)
        return remote(gsum, precv.at[q], p_send.at[tq], p_recv.at[q], device(tq, y, m))

    def p_wait(k):
        tq = lax.rem(q + k, n_pair)
        return remote(gsum, precv.at[tq], p_send.at[tq], p_recv.at[tq], device(tq, y, m))

    for k in range(1, n_pair):
        p_copy(k).start()
    precv[q] = total
    for k in range(1, n_pair):
        p_wait(k).wait_recv()
    total = precv[0]
    for k in range(1, n_pair):
        total = total + precv[k]
    own = pl.ds(pl.multiple_of(block * group, 8), block)
    gfull[own] = total

    def g_copy(other, ty, tm):
        return remote(gfull.at[own], gfull.at[own], g_send.at[other], g_recv.at[group], device(q, ty, tm))

    def g_wait(other, ty, tm):
        rows_there = gfull.at[pl.ds(pl.multiple_of(block * other, 8), block)]
        return remote(rows_there, rows_there, g_send.at[other], g_recv.at[other], device(q, ty, tm))

    for k in range(1, n_group):
        g_copy(*peer(k)).start()
    for k in range(1, n_group):
        g_wait(*peer(k)).wait_recv()

    ident = jnp.where(
        lax.broadcasted_iota(jnp.int32, (ens, ens), 0) == lax.broadcasted_iota(jnp.int32, (ens, ens), 1), 1.0, 0.0
    )
    matrix = ident + gfull[:, :ens]
    scale = jnp.sum(jnp.sum(matrix * ident, axis=1, keepdims=True), axis=0, keepdims=True)

    upper = matrix / scale
    factor = 1.5 * ident - 0.5 * upper
    upper, lower = dot(upper, factor), factor
    for _ in range(ROOT_ITERATIONS - 1):
        factor = 1.5 * ident - 0.5 * dot(lower, upper)
        upper, lower = dot(upper, factor), dot(factor, lower)
    mean_w = dot(lower, dot(lower, gfull[:, ens:])) / (scale * jnp.sqrt(jnp.float32(ens - 1.0)))
    total_w = lower / jnp.sqrt(scale) + mean_w
    omega = 1.0 / ens + total_w - jnp.sum(total_w, axis=0, keepdims=True) / ens
    turned = left_parts(omega.T)

    depth = rows // CHUNKS

    def b_copy(h, tm):
        return remote(
            mixed.at[pl.ds(depth * h, depth), pl.ds(pl.multiple_of(kd * tm, 8), kd)],
            out.at[pl.ds(depth * h, depth), :, pl.ds(pl.multiple_of(span * m, 128), span)],
            b_send.at[tm, h], b_recv.at[m, h], device(q, y, tm),
        )

    def b_wait(h, tm):
        return remote(
            mixed.at[pl.ds(depth * h, depth), pl.ds(0, kd)],
            out.at[pl.ds(depth * h, depth), :, pl.ds(pl.multiple_of(span * tm, 128), span)],
            b_send.at[tm, h], b_recv.at[tm, h], device(q, y, tm),
        )

    def b_keep(h):
        return pltpu.make_async_copy(
            mixed.at[pl.ds(depth * h, depth), pl.ds(pl.multiple_of(kd * m, 8), kd)],
            out.at[pl.ds(depth * h, depth), :, pl.ds(pl.multiple_of(span * m, 128), span)],
            b_send.at[m, h],
        )

    for h in range(CHUNKS):
        for row in range(depth * h, depth * h + depth):
            mixed[row] = product(turned, right_parts(fore[row]))
        for k in range(1, n_mem):
            b_copy(h, lax.rem(m + k, n_mem)).start()
        b_keep(h).start()

    geo_pair().wait_send()
    for c in range(octs):
        y_copy(c).wait_send()

    @pl.when(forward_edge)
    def _():
        for side in range(2):
            geo_side(side).wait_send()
        for c in range(octs):
            direct_copy(c).wait_send()

    for k in range(1, n_group):
        for c in range(octs):
            a_copy(c, *peer(k)).wait_send()
        s_copy(*peer(k)).wait_send()
        g_copy(*peer(k)).wait_send()
    for k in range(1, n_pair):
        p_copy(k).wait_send()
    for h in range(CHUNKS):
        b_keep(h).wait()
        for k in range(1, n_mem):
            b_copy(h, lax.rem(m + k, n_mem)).wait_send()
            b_wait(h, lax.rem(m + k, n_mem)).wait_recv()


def local(n_slab, n_mem, states, land_mask, cell_class, kappa, flow, obs_index, obs_values, obs_var):
    kd, rows, lon = states.shape
    ens = kd * n_mem
    n_pair, n_group, octs = n_slab // 2, 2 * n_mem, kd // 16
    span, block = lon // n_mem, ens // n_group
    n_obs = obs_index.shape[0]
    swapped = states.reshape(kd // 8, 8, rows, lon).transpose(0, 2, 1, 3)
    geo = jnp.stack([cell_class, land_mask])
    dma = pltpu.SemaphoreType.DMA
    vmem = pl.BlockSpec(memory_space=pltpu.VMEM)
    smem = pl.BlockSpec(memory_space=pltpu.SMEM)
    f32 = jnp.float32
    out = pl.pallas_call(
        functools.partial(cycle_kernel, n_slab, n_mem),
        out_shape=jax.ShapeDtypeStruct((rows, kd, lon), f32),
        in_specs=[vmem, vmem, smem, smem, vmem, vmem, vmem],
        out_specs=vmem,
        scratch_shapes=[
            pltpu.VMEM((2, octs, 4 * rows, 8, lon), f32),
            pltpu.VMEM((4 * rows, 5, 8, lon), f32),
            pltpu.VMEM((4, 2, rows, lon), jnp.int32),
            pltpu.VMEM((rows, ens, span), f32),
            pltpu.VMEM((rows, ens, span), f32),
            pltpu.VMEM((ens, 2 * ens), f32),
            pltpu.VMEM((n_group, block, 2 * ens), f32),
            pltpu.VMEM((block, 2 * ens), f32),
            pltpu.VMEM((n_pair, block, 2 * ens), f32),
            pltpu.VMEM((ens, 2 * ens), f32),
            dma((3,)), dma((4,)), dma((octs,)), dma((octs,)), dma((octs,)), dma((octs,)),
            dma((2, octs)), dma((octs,)),
            dma((n_group, octs)), dma((n_group, octs)),
            dma((n_group,)), dma((n_group,)), dma((n_pair,)), dma((n_pair,)),
            dma((n_group,)), dma((n_group,)), dma((n_mem, CHUNKS)), dma((n_mem, CHUNKS)),
        ],
        compiler_params=pltpu.CompilerParams(
            collective_id=0, has_side_effects=True, vmem_limit_bytes=40 * 1024 * 1024
        ),
        name="cycle",
    )(
        swapped, geo, kappa, flow,
        obs_index.reshape(1, n_obs), obs_values.reshape(1, n_obs), obs_var.reshape(1, n_obs),
    )
    return out.transpose(1, 0, 2)


def solution(mesh):
    return jax.shard_map(
        functools.partial(local, mesh.shape["slab"], mesh.shape["mem"]),
        mesh=mesh,
        in_specs=(
            P("mem", "slab", None),
            P("slab", None),
            P("slab", None),
            P(),
            P(),
            P("slab"),
            P("slab"),
            P("slab"),
        ),
        out_specs=P("mem", "slab", None),
        check_vma=False,
    )
```

time: 310 us -> 95.4 us (0.31)
  waiting for transfers between devices: 105 us -> 0 us
  Pallas kernels: 0 us -> 89.9 us
  blocking collectives: 62.9 us -> 0 us
  starting transfers between devices: 58.4 us -> 0 us
  other arithmetic: 26.7 us -> 0.78 us
  local copies, waits for them, and re-layouts: 29.9 us -> 4.09 us
  between operations: 15.3 us -> 0.07 us
  matrix products: 10.1 us -> 0 us
    pallas_call x0 -> x1, Pallas kernels: none -> 89.9 us  [local(): pl.pallas_call(functools.partial(cycle_kernel, n_slab, n_mem), out_shape=...]
    psum x1 -> x0, waiting for transfers between devices: 76.2 us -> none  [local(): gram, proj = lax.psum((gram_part, proj_part), ('slab', 'mem'))]
    ppermute x16 -> x0, starting transfers between devices: 51.4 us -> none  [the longest x8 41.1 us: extended(): lax.ppermute(lax.slice_in_dim(block, block.shape[dim] - width, None, axis...]
    psum x1 -> x0, blocking collectives: 44.7 us -> none  [local(): gram, proj = lax.psum((gram_part, proj_part), ('slab', 'mem'))]
    ppermute x16 -> x0, waiting for transfers between devices: 29.1 us -> none  [the longest x8 20.7 us: extended(): lax.ppermute(lax.slice_in_dim(block, block.shape[dim] - width, None, axis...]
    all_to_all x1 -> x0, blocking collectives: 18.2 us -> none  [local(): return lax.all_to_all(mixed, 'mem', split_axis=0, concat_axis=2, tiled=True)]
    mul x10 -> x0, other arithmetic: 15.3 us -> none  [the longest x8 5.25 us: advance(): wet_cells * (center + diffusion * spread - 0.5 * flow_east * (east - west...]
    unnamed x19 -> x10, local copies, waits for them, and re-layouts: 10.9 us -> 0.65 us
  transfers between devices with their start and end apart: 19 -> 0, of which waited for: 15 -> 0; matrix products, arithmetic and copies ran while one was open for 13% -> 0% of each run, Pallas kernels for 0% -> 0%
where the time goes in v1:
time: 95.4 us; the launch traced here: 94.9 us
  Pallas kernels  89.9 us (94%)
  local copies, waits for them, and re-layouts  4.09 us (4%)
    pallas_call x1, Pallas kernels, local(): pl.pallas_call(functools.partial(cycle_kernel, n_slab, n_mem), out_shape=...  89.9 us

profile of v1, /device:TPU:0, one launch (start us, length us, event | category | flops | bytes accessed | tf_op | source)
XLA Modules:
  0.0 94.9 jit_solution(17638584854180767212)
XLA Ops:
  0.0 0.8 pad_add_fusion.geo
  0.8 0.0 copy-start.2
  0.8 0.0 copy-start.3
  0.8 0.0 copy-start.4
  0.8 1.9 %copy.13 = f32[4,8,8,1024]{3,1,2,0:T(8,128)S(1)} copy(f32[4,8,8,1024]{3,2,1,0:T(8,128)} %bitcast.15) | data formatting | bytes 2097152 | tf_op jit(solution)/shard_map/reshape | solution.py:423
  2.7 0.0 copy-start
  2.7 0.0 copy-start.1
  2.7 0.0 copy-done.2
  2.7 0.0 copy-done.3
  2.7 0.0 copy-done.4
  2.7 0.6 copy-done
  3.3 0.0 copy-done.1
  3.4 89.9 %cycle.1 = f32[8,32,1024]{2,1,0:T(8,128)S(1)} custom-call(f32[4,8,8,1024]{3,2,1,0:T(8,128)S(1)} %bitcast.11, s32[2,8,1024]{2,1,0:T(8,128)S(1)} %pad_add_fusion.geo, f32[8]{0:T(128)S(1)} %copy-done.1, f32[2,8]{1,0:T(2,128)S(1)} %copy-done, s32[1,128]{1,0:T(1,128)S(1)} %bitcast.12, f32[1,128]{1,0:T(1,128)S(1)} %bitcast.13, f32[1,128]{1,0:T(1,128)S(1)} %bitcast.14), custom_call_target="tpu_custom_call" | custom-call | tf_op jit(solution)/shard_map/cycle/pallas_call | solution.py:429
  93.3 1.6 %copy.11 = f32[32,8,1024]{2,1,0:T(8,128)} copy(f32[32,8,1024]{2,0,1:T(8,128)S(1)} %bitcast.10) | data formatting | bytes 2097152 | tf_op jit(solution)/shard_map/transpose | solution.py:459
Async XLA Ops:
  0.8 1.9 %copy-start.2 = (s32[128]{0:T(128)S(1)}, s32[128]{0:T(128)}, u32[]{:S(2)}) copy-start(s32[128]{0:T(128)} %param.13) | copy-start | bytes 1540
  0.8 1.9 %copy-start.3 = (f32[128]{0:T(128)S(1)}, f32[128]{0:T(128)}, u32[]{:S(2)}) copy-start(f32[128]{0:T(128)} %param.14) | copy-start | bytes 1540
  0.8 1.9 %copy-start.4 = (f32[128]{0:T(128)S(1)}, f32[128]{0:T(128)}, u32[]{:S(2)}) copy-start(f32[128]{0:T(128)} %param.15) | copy-start | bytes 1540
  2.7 0.7 copy-start
  2.7 0.7 copy-start.1

commit v2 on v1

--- a/solution.py
+++ b/solution.py
@@ -11,6 +11,7 @@
 ROOT_ITERATIONS = 8
 NCLS = 8
 CHUNKS = 4
+HEIGHT = 4
 
 
 def halves(x):
@@ -40,7 +41,7 @@
     n_slab, n_mem,
     states, geo, kappa, flow, obs_index, obs_values, obs_var,
     out,
-    buf, coef, geos, fore, mixed, gpart, grecv, gsum, precv, gfull,
+    buf, coef, geos, fore, mixed, gpart, grecv, gsum, precv, gfull, turned,
     geo_send, geo_recv, y_send, y_recv, d_send, r_send, z_recv, keep_sem,
     a_send, a_recv, s_send, s_recv, p_send, p_recv, g_send, g_recv, b_send, b_recv,
 ):
@@ -50,12 +51,19 @@
     n_pair, n_group = n_slab // 2, 2 * n_mem
     octs, rows, _, lon = states.shape[0] // 2, states.shape[1], states.shape[2], states.shape[3]
     span = lon // n_mem
-    ens = fore.shape[1]
+    ens = fore.shape[2]
+    n_line, line, core = n_mem // 2, lax.div(m, 2), lax.rem(m, 2)
     block = ens // n_group
     kd = octs * 16
     group = y * n_mem + m
     last = n_pair - 1
     step_pair = 2 * y - 1
+
+    def quarter(member, j):
+        return lax.rem(member, 2) * n_line + lax.rem(lax.div(member, 2) + j, n_line)
+
+    def start_at(member, j):
+        return pl.multiple_of(span * quarter(member, j), 128)
 
     def device(pair, side, member):
         return (2 * pair + side, member)
@@ -199,26 +207,32 @@
 
     lax.fori_loop(0, 4, coefficients, 0)
 
-    def a_copy(c, other, ty, tm):
-        return remote(
-            buf.at[0, c, pl.ds(8 + 8 * ty, 8), :, pl.ds(pl.multiple_of(span * tm, 128), span)],
-            fore.at[:, pl.ds(pl.multiple_of(kd * m + 8 * octs * y + 8 * c, 8), 8), :],
-            a_send.at[other, c], a_recv.at[group, c], device(q, ty, tm),
-        )
-
-    def a_wait(c, other, ty, tm):
+    def a_copy(j, c, other, ty, tm):
+        return remote(
+            buf.at[0, c, pl.ds(8 + 8 * ty, 8), :, pl.ds(start_at(tm, j), span)],
+            fore.at[j, :, pl.ds(pl.multiple_of(kd * m + 8 * octs * y + 8 * c, 8), 8), :],
+            a_send.at[j, other, c], a_recv.at[j, group, c], device(q, ty, tm),
+        )
+
+    def a_wait(j, c, other, ty, tm):
         return remote(
             buf.at[0, c, pl.ds(8, 8), :, pl.ds(0, span)],
-            fore.at[:, pl.ds(pl.multiple_of(kd * tm + 8 * octs * ty + 8 * c, 8), 8), :],
-            a_send.at[other, c], a_recv.at[other, c], device(q, ty, tm),
-        )
-
-    def a_keep(c):
+            fore.at[j, :, pl.ds(pl.multiple_of(kd * tm + 8 * octs * ty + 8 * c, 8), 8), :],
+            a_send.at[j, other, c], a_recv.at[j, other, c], device(q, ty, tm),
+        )
+
+    def a_keep(j, c):
         return pltpu.make_async_copy(
-            buf.at[0, c, pl.ds(8 + 8 * y, 8), :, pl.ds(pl.multiple_of(span * m, 128), span)],
-            fore.at[:, pl.ds(pl.multiple_of(kd * m + 8 * octs * y + 8 * c, 8), 8), :],
-            a_send.at[group, c],
-        )
+            buf.at[0, c, pl.ds(8 + 8 * y, 8), :, pl.ds(start_at(m, j), span)],
+            fore.at[j, :, pl.ds(pl.multiple_of(kd * m + 8 * octs * y + 8 * c, 8), 8), :],
+            a_send.at[j, group, c],
+        )
+
+    def rest_start(c):
+        for j in range(1, n_line):
+            for k in range(1, n_group):
+                a_copy(j, c, *peer(k)).start()
+            a_keep(j, c).start()
 
     for c in range(octs):
         keep(c).wait()
@@ -239,45 +253,51 @@
             for parity in range(2):
                 t = 2 * pair_step + parity
 
-                def advance(r, inner):
-                    center = buf[parity, c, r]
-                    east = pltpu.roll(center, lon - 1, 1)
-                    west = pltpu.roll(center, 1, 1)
-                    buf[1 - parity, c, r] = (
-                        coef[r, 0] * center
-                        + coef[r, 1] * buf[parity, c, r + 1]
-                        + coef[r, 2] * buf[parity, c, r - 1]
-                        + coef[r, 3] * east
-                        + coef[r, 4] * west
-                    )
-                    return inner
-
-                lax.fori_loop(t + 1, 31 - t, advance, 0)
+                def advance(height, first, g):
+                    base = first + height * g
+                    level = [buf[parity, c, base - 1 + k] for k in range(height + 2)]
+                    fresh = []
+                    for k in range(height):
+                        center = level[k + 1]
+                        fresh.append(
+                            coef[base + k, 0] * center
+                            + coef[base + k, 1] * level[k + 2]
+                            + coef[base + k, 2] * level[k]
+                            + coef[base + k, 3] * pltpu.roll(center, lon - 1, 1)
+                            + coef[base + k, 4] * pltpu.roll(center, 1, 1)
+                        )
+                    for k in range(height):
+                        buf[1 - parity, c, base + k] = fresh[k]
+
+                lax.fori_loop(0, (30 - 2 * t) // HEIGHT, lambda g, inner: (advance(HEIGHT, t + 1, g), inner)[1], 0)
+                if HEIGHT == 4 and parity == 0:
+                    advance(2, 29 - t, 0)
             return carry
 
         lax.fori_loop(0, STEPS // 2, two_steps, 0)
         for k in range(1, n_group):
-            a_copy(c, *peer(k)).start()
-        a_keep(c).start()
+            a_copy(0, c, *peer(k)).start()
+        a_keep(0, c).start()
+        rest_start(c)
 
     for c in range(octs):
-        a_keep(c).wait()
+        a_keep(0, c).wait()
         for k in range(1, n_group):
-            a_wait(c, *peer(k)).wait_recv()
+            a_wait(0, c, *peer(k)).wait_recv()
 
     place = obs_index[...]
     n_obs = place.shape[1]
     hx = jnp.zeros((ens, n_obs), jnp.float32)
-    inner = lax.broadcasted_iota(jnp.int32, (span, n_obs), 0) + span * m
+    inner = lax.broadcasted_iota(jnp.int32, (span, n_obs), 0) + start_at(m, 0)
     for row in range(rows):
         pick = jnp.where(inner + row * lon == place, 1.0, 0.0).astype(jnp.bfloat16)
-        rest = fore[row]
+        rest = fore[0, row]
         for _ in range(3):
             part = rest.astype(jnp.bfloat16)
             hx = hx + jnp.dot(part, pick, preferred_element_type=jnp.float32)
             rest = rest - part.astype(jnp.float32)
     column = place & (lon - 1)
-    mine = (column >= span * m) & (column < span * m + span)
+    mine = (column >= start_at(m, 0)) & (column < start_at(m, 0) + span)
     ybar = jnp.sum(hx, axis=0, keepdims=True) / ens
     err = obs_var[...] * (1.0 + 2.0 * s.astype(jnp.float32) / float(n_slab - 1))
     anom = jnp.where(mine, (hx - ybar) / jnp.sqrt(err * (ens - 1.0)), 0.0)
@@ -357,37 +377,42 @@
     mean_w = dot(lower, dot(lower, gfull[:, ens:])) / (scale * jnp.sqrt(jnp.float32(ens - 1.0)))
     total_w = lower / jnp.sqrt(scale) + mean_w
     omega = 1.0 / ens + total_w - jnp.sum(total_w, axis=0, keepdims=True) / ens
-    turned = left_parts(omega.T)
+    turned[...] = omega.T
+    sibling = 2 * line + 1 - core
+    weights = left_parts(
+        jnp.concatenate(
+            [turned[pl.ds(pl.multiple_of(kd * m, 8), kd)], turned[pl.ds(pl.multiple_of(kd * sibling, 8), kd)]], axis=0
+        )
+    )
 
     depth = rows // CHUNKS
 
-    def b_copy(h, tm):
-        return remote(
-            mixed.at[pl.ds(depth * h, depth), pl.ds(pl.multiple_of(kd * tm, 8), kd)],
-            out.at[pl.ds(depth * h, depth), :, pl.ds(pl.multiple_of(span * m, 128), span)],
-            b_send.at[tm, h], b_recv.at[m, h], device(q, y, tm),
-        )
-
-    def b_wait(h, tm):
-        return remote(
-            mixed.at[pl.ds(depth * h, depth), pl.ds(0, kd)],
-            out.at[pl.ds(depth * h, depth), :, pl.ds(pl.multiple_of(span * tm, 128), span)],
-            b_send.at[tm, h], b_recv.at[tm, h], device(q, y, tm),
-        )
-
-    def b_keep(h):
-        return pltpu.make_async_copy(
-            mixed.at[pl.ds(depth * h, depth), pl.ds(pl.multiple_of(kd * m, 8), kd)],
-            out.at[pl.ds(depth * h, depth), :, pl.ds(pl.multiple_of(span * m, 128), span)],
-            b_send.at[m, h],
-        )
-
-    for h in range(CHUNKS):
-        for row in range(depth * h, depth * h + depth):
-            mixed[row] = product(turned, right_parts(fore[row]))
-        for k in range(1, n_mem):
-            b_copy(h, lax.rem(m + k, n_mem)).start()
-        b_keep(h).start()
+    def b_copy(j, h):
+        return remote(
+            mixed.at[j, pl.ds(depth * h, depth)],
+            out.at[pl.ds(depth * h, depth), :, pl.ds(start_at(m, j), span)],
+            b_send.at[j, h], b_recv.at[j, h], device(q, y, sibling),
+        )
+
+    def b_wait(j, h):
+        return remote(
+            mixed.at[j, pl.ds(depth * h, depth)],
+            out.at[pl.ds(depth * h, depth), :, pl.ds(start_at(sibling, j), span)],
+            b_send.at[j, h], b_recv.at[j, h], device(q, y, sibling),
+        )
+
+    for j in range(n_line):
+        if j > 0:
+            for c in range(octs):
+                a_keep(j, c).wait()
+                for k in range(1, n_group):
+                    a_wait(j, c, *peer(k)).wait_recv()
+        for h in range(CHUNKS):
+            for row in range(depth * h, depth * h + depth):
+                result = product(weights, right_parts(fore[j, row]))
+                mixed[j, row] = result[kd:]
+                out[row, :, pl.ds(start_at(m, j), span)] = result[:kd]
+            b_copy(j, h).start()
 
     geo_pair().wait_send()
     for c in range(octs):
@@ -402,22 +427,22 @@
 
     for k in range(1, n_group):
         for c in range(octs):
-            a_copy(c, *peer(k)).wait_send()
+            for j in range(n_line):
+                a_copy(j, c, *peer(k)).wait_send()
         s_copy(*peer(k)).wait_send()
         g_copy(*peer(k)).wait_send()
     for k in range(1, n_pair):
         p_copy(k).wait_send()
-    for h in range(CHUNKS):
-        b_keep(h).wait()
-        for k in range(1, n_mem):
-            b_copy(h, lax.rem(m + k, n_mem)).wait_send()
-            b_wait(h, lax.rem(m + k, n_mem)).wait_recv()
+    for j in range(n_line):
+        for h in range(CHUNKS):
+            b_copy(j, h).wait_send()
+            b_wait(j, h).wait_recv()
 
 
 def local(n_slab, n_mem, states, land_mask, cell_class, kappa, flow, obs_index, obs_values, obs_var):
     kd, rows, lon = states.shape
     ens = kd * n_mem
-    n_pair, n_group, octs = n_slab // 2, 2 * n_mem, kd // 16
+    n_pair, n_group, n_line, octs = n_slab // 2, 2 * n_mem, n_mem // 2, kd // 16
     span, block = lon // n_mem, ens // n_group
     n_obs = obs_index.shape[0]
     swapped = states.reshape(kd // 8, 8, rows, lon).transpose(0, 2, 1, 3)
@@ -435,18 +460,19 @@
             pltpu.VMEM((2, octs, 4 * rows, 8, lon), f32),
             pltpu.VMEM((4 * rows, 5, 8, lon), f32),
             pltpu.VMEM((4, 2, rows, lon), jnp.int32),
-            pltpu.VMEM((rows, ens, span), f32),
-            pltpu.VMEM((rows, ens, span), f32),
+            pltpu.VMEM((n_line, rows, ens, span), f32),
+            pltpu.VMEM((n_line, rows, kd, span), f32),
             pltpu.VMEM((ens, 2 * ens), f32),
             pltpu.VMEM((n_group, block, 2 * ens), f32),
             pltpu.VMEM((block, 2 * ens), f32),
             pltpu.VMEM((n_pair, block, 2 * ens), f32),
             pltpu.VMEM((ens, 2 * ens), f32),
+            pltpu.VMEM((ens, ens), f32),
             dma((3,)), dma((4,)), dma((octs,)), dma((octs,)), dma((octs,)), dma((octs,)),
             dma((2, octs)), dma((octs,)),
-            dma((n_group, octs)), dma((n_group, octs)),
+            dma((n_line, n_group, octs)), dma((n_line, n_group, octs)),
             dma((n_group,)), dma((n_group,)), dma((n_pair,)), dma((n_pair,)),
-            dma((n_group,)), dma((n_group,)), dma((n_mem, CHUNKS)), dma((n_mem, CHUNKS)),
+            dma((n_group,)), dma((n_group,)), dma((n_line, CHUNKS)), dma((n_line, CHUNKS)),
         ],
         compiler_params=pltpu.CompilerParams(
             collective_id=0, has_side_effects=True, vmem_limit_bytes=40 * 1024 * 1024

time: 95.4 us -> 73.6 us (0.77)
  Pallas kernels: 89.9 us -> 68.5 us
    pallas_call x1, Pallas kernels: 89.9 us -> 68.5 us  [local(): pl.pallas_call(functools.partial(cycle_kernel, n_slab, n_mem), out_shape=...]
where the time goes in v2:
time: 73.6 us; the launch traced here: 73.4 us
  Pallas kernels  68.5 us (93%)
  local copies, waits for them, and re-layouts  4.09 us (6%)
  other arithmetic  0.78 us (1%)
    pallas_call x1, Pallas kernels, local(): pl.pallas_call(functools.partial(cycle_kernel, n_slab, n_mem), out_shape=...  68.5 us
    reshape x1, local copies, waits for them, and re-layouts, local(): swapped = states.reshape(kd // 8, 8, rows, lon).transpose(0, 2, 1, 3)  1.86 us
    transpose x1, local copies, waits for them, and re-layouts, local(): return out.transpose(1, 0, 2)  1.58 us

profile of v2, /device:TPU:0, one launch (start us, length us, event | category | flops | bytes accessed | tf_op | source)
XLA Modules:
  0.0 73.4 jit_solution(2752960477809442383)
XLA Ops:
  0.0 0.8 %pad_add_fusion.geo = s32[2,8,1024]{2,1,0:T(8,128)S(1)} fusion(s32[1,8,1024]{2,1,0:T(8,128)} %bitcast.16, s32[1,8,1024]{2,1,0:T(8,128)} %bitcast.17), kind=kLoop, calls=%fused_computation.1 | loop fusion | flops 16384 | bytes 131072 | tf_op jit(solution)/shard_map/stack | solution.py:449
  0.8 0.0 copy-start.2
  0.8 0.0 copy-start.3
  0.8 0.0 copy-start.4
  0.8 1.9 %copy.13 = f32[4,8,8,1024]{3,1,2,0:T(8,128)S(1)} copy(f32[4,8,8,1024]{3,2,1,0:T(8,128)} %bitcast.15) | data formatting | bytes 2097152 | tf_op jit(solution)/shard_map/reshape | solution.py:448
  2.7 0.0 copy-start
  2.7 0.0 copy-start.1
  2.7 0.0 copy-done.2
  2.7 0.0 copy-done.3
  2.7 0.0 copy-done.4
  2.7 0.6 copy-done
  3.3 0.0 copy-done.1
  3.4 68.5 %cycle.1 = f32[8,32,1024]{2,1,0:T(8,128)S(1)} custom-call(f32[4,8,8,1024]{3,2,1,0:T(8,128)S(1)} %bitcast.11, s32[2,8,1024]{2,1,0:T(8,128)S(1)} %pad_add_fusion.geo, f32[8]{0:T(128)S(1)} %copy-done.1, f32[2,8]{1,0:T(2,128)S(1)} %copy-done, s32[1,128]{1,0:T(1,128)S(1)} %bitcast.12, f32[1,128]{1,0:T(1,128)S(1)} %bitcast.13, f32[1,128]{1,0:T(1,128)S(1)} %bitcast.14), custom_call_target="tpu_custom_call" | custom-call | tf_op jit(solution)/shard_map/cycle/pallas_call | solution.py:454
  71.8 1.6 %copy.11 = f32[32,8,1024]{2,1,0:T(8,128)} copy(f32[32,8,1024]{2,0,1:T(8,128)S(1)} %bitcast.10) | data formatting | bytes 2097152 | tf_op jit(solution)/shard_map/transpose | solution.py:485
Async XLA Ops:
  0.8 1.9 %copy-start.2 = (s32[128]{0:T(128)S(1)}, s32[128]{0:T(128)}, u32[]{:S(2)}) copy-start(s32[128]{0:T(128)} %param.13) | copy-start | bytes 1540
  0.8 1.9 %copy-start.3 = (f32[128]{0:T(128)S(1)}, f32[128]{0:T(128)}, u32[]{:S(2)}) copy-start(f32[128]{0:T(128)} %param.14) | copy-start | bytes 1540
  0.8 1.9 %copy-start.4 = (f32[128]{0:T(128)S(1)}, f32[128]{0:T(128)}, u32[]{:S(2)}) copy-start(f32[128]{0:T(128)} %param.15) | copy-start | bytes 1540
  2.7 0.7 copy-start
  2.7 0.7 copy-start.1

commit v3 on v2

--- a/solution.py
+++ b/solution.py
@@ -12,6 +12,7 @@
 NCLS = 8
 CHUNKS = 4
 HEIGHT = 4
+SPLIT = 2
 
 
 def halves(x):
@@ -39,7 +40,7 @@
 
 def cycle_kernel(
     n_slab, n_mem,
-    states, geo, kappa, flow, obs_index, obs_values, obs_var,
+    states, classes_in, mask_in, kappa, flow, obs_index, obs_values, obs_var,
     out,
     buf, coef, geos, fore, mixed, gpart, grecv, gsum, precv, gfull, turned,
     geo_send, geo_recv, y_send, y_recv, d_send, r_send, z_recv, keep_sem,
@@ -88,47 +89,53 @@
             pl.semaphore_signal(barrier, inc=1, device_id=device(tq, side, m), device_id_type=pl.DeviceIdType.MESH)
     pl.semaphore_wait(barrier, n_group - 1 + 2 * (n_pair - 1))
 
-    def y_copy(c):
-        return remote(
-            states.at[octs * (1 - y) + c], buf.at[0, c, pl.ds(8 + 8 * y, 8)],
-            y_send.at[c], y_recv.at[c], device(q, 1 - y, m),
-        )
-
-    def y_wait(c):
-        return remote(
-            states.at[c], buf.at[0, c, pl.ds(16 - 8 * y, 8)],
-            y_send.at[c], y_recv.at[c], device(q, 1 - y, m),
-        )
-
-    def direct_copy(c):
-        return remote(
-            states.at[octs * y + c], buf.at[0, c, pl.ds(24 * (1 - y), 8)],
-            d_send.at[c], z_recv.at[1 - y, c], device(q + step_pair, y, m),
-        )
-
-    def relay_copy(c):
-        return remote(
-            buf.at[0, c, pl.ds(16 - 8 * y, 8)], buf.at[0, c, pl.ds(24 * y, 8)],
-            r_send.at[c], z_recv.at[y, c], device(q - step_pair, y, m),
-        )
-
-    def z_wait(side, c):
-        return remote(
-            states.at[c], buf.at[0, c, pl.ds(24 * side, 8)],
-            d_send.at[c], z_recv.at[side, c], device(q, 1 - y, m),
-        )
-
-    def geo_pair():
-        return remote(geo, geos.at[1 + y], geo_send.at[0], geo_recv.at[1 + y], device(q, 1 - y, m))
-
-    def geo_side(side):
-        return remote(
-            geo, geos.at[3 * (1 - y)], geo_send.at[1 + side], geo_recv.at[3 * (1 - y)],
+    piece = 8 // SPLIT
+
+    def y_copy(c, h):
+        return remote(
+            states.at[octs * (1 - y) + c, pl.ds(piece * h, piece)], buf.at[0, c, pl.ds(8 + 8 * y + piece * h, piece)],
+            y_send.at[c, h], y_recv.at[c, h], device(q, 1 - y, m),
+        )
+
+    def y_wait(c, h):
+        return remote(
+            states.at[c, pl.ds(0, piece)], buf.at[0, c, pl.ds(16 - 8 * y + piece * h, piece)],
+            y_send.at[c, h], y_recv.at[c, h], device(q, 1 - y, m),
+        )
+
+    def direct_copy(c, h):
+        return remote(
+            states.at[octs * y + c, pl.ds(piece * h, piece)], buf.at[0, c, pl.ds(24 * (1 - y) + piece * h, piece)],
+            d_send.at[c, h], z_recv.at[1 - y, c, h], device(q + step_pair, y, m),
+        )
+
+    def relay_copy(c, h):
+        return remote(
+            buf.at[0, c, pl.ds(16 - 8 * y + piece * h, piece)], buf.at[0, c, pl.ds(24 * y + piece * h, piece)],
+            r_send.at[c, h], z_recv.at[y, c, h], device(q - step_pair, y, m),
+        )
+
+    def z_wait(side, c, h):
+        return remote(
+            states.at[c, pl.ds(0, piece)], buf.at[0, c, pl.ds(24 * side + piece * h, piece)],
+            d_send.at[c, h], z_recv.at[side, c, h], device(q, 1 - y, m),
+        )
+
+    fields = (classes_in, mask_in)
+
+    def geo_pair(f):
+        return remote(
+            fields[f], geos.at[1 + y, f], geo_send.at[0, f], geo_recv.at[1 + y, f], device(q, 1 - y, m)
+        )
+
+    def geo_side(side, f):
+        return remote(
+            fields[f], geos.at[3 * (1 - y), f], geo_send.at[1 + side, f], geo_recv.at[3 * (1 - y), f],
             device(q + step_pair, side, m),
         )
 
-    def geo_wait(slot):
-        return remote(geo, geos.at[slot], geo_send.at[0], geo_recv.at[slot], device(q, 1 - y, m))
+    def geo_wait(slot, f):
+        return remote(fields[f], geos.at[slot, f], geo_send.at[0, f], geo_recv.at[slot, f], device(q, 1 - y, m))
 
     def keep(c):
         return pltpu.make_async_copy(states.at[octs * y + c], buf.at[0, c, pl.ds(8 + 8 * y, 8)], keep_sem.at[c])
@@ -136,20 +143,25 @@
     forward_edge = (q + step_pair >= 0) & (q + step_pair <= last)
     backward_edge = (q - step_pair >= 0) & (q - step_pair <= last)
 
-    geo_pair().start()
+    for f in range(2):
+        geo_pair(f).start()
     for c in range(octs):
-        y_copy(c).start()
+        for h in range(SPLIT):
+            y_copy(c, h).start()
 
     @pl.when(forward_edge)
     def _():
         for side in range(2):
-            geo_side(side).start()
+            for f in range(2):
+                geo_side(side, f).start()
         for c in range(octs):
-            direct_copy(c).start()
+            for h in range(SPLIT):
+                direct_copy(c, h).start()
 
     for c in range(octs):
         keep(c).start()
-    geos[1 + y] = geo[...]
+    for f in range(2):
+        geos[1 + y, f] = fields[f][...]
 
     @pl.when(q == 0)
     def _():
@@ -164,21 +176,25 @@
             buf[0, c, 24:32] = jnp.zeros((8, 8, lon), jnp.float32)
 
     for c in range(octs):
-        y_wait(c).wait_recv()
-
-        @pl.when(backward_edge)
-        def _():
-            relay_copy(c).start()
-
-    geo_wait(2 - y).wait_recv()
+        for h in range(SPLIT):
+            y_wait(c, h).wait_recv()
+
+            @pl.when(backward_edge)
+            def _():
+                relay_copy(c, h).start()
+
+    for f in range(2):
+        geo_wait(2 - y, f).wait_recv()
 
     @pl.when(q > 0)
     def _():
-        geo_wait(0).wait_recv()
+        for f in range(2):
+            geo_wait(0, f).wait_recv()
 
     @pl.when(q < last)
     def _():
-        geo_wait(3).wait_recv()
+        for f in range(2):
+            geo_wait(3, f).wait_recv()
 
     lane = lax.broadcasted_iota(jnp.int32, (8, lon), 1)
 
@@ -239,15 +255,18 @@
 
         @pl.when(q > 0)
         def _():
-            z_wait(0, c).wait_recv()
+            for h in range(SPLIT):
+                z_wait(0, c, h).wait_recv()
 
         @pl.when(q < last)
         def _():
-            z_wait(1, c).wait_recv()
+            for h in range(SPLIT):
+                z_wait(1, c, h).wait_recv()
 
         @pl.when(backward_edge)
         def _():
-            relay_copy(c).wait_send()
+            for h in range(SPLIT):
+                relay_copy(c, h).wait_send()
 
         def two_steps(pair_step, carry):
             for parity in range(2):
@@ -278,7 +297,8 @@
         for k in range(1, n_group):
             a_copy(0, c, *peer(k)).start()
         a_keep(0, c).start()
-        rest_start(c)
+        if c < octs - 1:
+            rest_start(c)
 
     for c in range(octs):
         a_keep(0, c).wait()
@@ -323,6 +343,7 @@
 
     for k in range(1, n_group):
         s_copy(*peer(k)).start()
+    rest_start(octs - 1)
     grecv[group] = gpart[pl.ds(pl.multiple_of(block * group, 8), block)]
     for k in range(1, n_group):
         s_wait(*peer(k)).wait_recv()
@@ -414,16 +435,20 @@
                 out[row, :, pl.ds(start_at(m, j), span)] = result[:kd]
             b_copy(j, h).start()
 
-    geo_pair().wait_send()
+    for f in range(2):
+        geo_pair(f).wait_send()
     for c in range(octs):
-        y_copy(c).wait_send()
+        for h in range(SPLIT):
+            y_copy(c, h).wait_send()
 
     @pl.when(forward_edge)
     def _():
         for side in range(2):
-            geo_side(side).wait_send()
+            for f in range(2):
+                geo_side(side, f).wait_send()
         for c in range(octs):
-            direct_copy(c).wait_send()
+            for h in range(SPLIT):
+                direct_copy(c, h).wait_send()
 
     for k in range(1, n_group):
         for c in range(octs):
@@ -446,7 +471,6 @@
     span, block = lon // n_mem, ens // n_group
     n_obs = obs_index.shape[0]
     swapped = states.reshape(kd // 8, 8, rows, lon).transpose(0, 2, 1, 3)
-    geo = jnp.stack([cell_class, land_mask])
     dma = pltpu.SemaphoreType.DMA
     vmem = pl.BlockSpec(memory_space=pltpu.VMEM)
     smem = pl.BlockSpec(memory_space=pltpu.SMEM)
@@ -454,7 +478,7 @@
     out = pl.pallas_call(
         functools.partial(cycle_kernel, n_slab, n_mem),
         out_shape=jax.ShapeDtypeStruct((rows, kd, lon), f32),
-        in_specs=[vmem, vmem, smem, smem, vmem, vmem, vmem],
+        in_specs=[vmem, vmem, vmem, smem, smem, vmem, vmem, vmem],
         out_specs=vmem,
         scratch_shapes=[
             pltpu.VMEM((2, octs, 4 * rows, 8, lon), f32),
@@ -468,8 +492,8 @@
             pltpu.VMEM((n_pair, block, 2 * ens), f32),
             pltpu.VMEM((ens, 2 * ens), f32),
             pltpu.VMEM((ens, ens), f32),
-            dma((3,)), dma((4,)), dma((octs,)), dma((octs,)), dma((octs,)), dma((octs,)),
-            dma((2, octs)), dma((octs,)),
+            dma((3, 2)), dma((4, 2)), dma((octs, SPLIT)), dma((octs, SPLIT)), dma((octs, SPLIT)), dma((octs, SPLIT)),
+            dma((2, octs, SPLIT)), dma((octs,)),
             dma((n_line, n_group, octs)), dma((n_line, n_group, octs)),
             dma((n_group,)), dma((n_group,)), dma((n_pair,)), dma((n_pair,)),
             dma((n_group,)), dma((n_group,)), dma((n_line, CHUNKS)), dma((n_line, CHUNKS)),
@@ -479,7 +503,7 @@
         ),
         name="cycle",
     )(
-        swapped, geo, kappa, flow,
+        swapped, cell_class, land_mask, kappa, flow,
         obs_index.reshape(1, n_obs), obs_values.reshape(1, n_obs), obs_var.reshape(1, n_obs),
     )
     return out.transpose(1, 0, 2)

time: 73.6 us -> 69.8 us (0.948)
  Pallas kernels: 68.5 us -> 65.4 us
  other arithmetic: 0.78 us -> 0 us
    pallas_call x1, Pallas kernels: 68.5 us -> 65.4 us  [local(): pl.pallas_call(functools.partial(cycle_kernel, n_slab, n_mem), out_shape=...]
    another operation x1 -> x0, other arithmetic: 0.78 us -> none  [local(): geo = jnp.stack([cell_class, land_mask])]
where the time goes in v3:
time: 69.8 us; the launch traced here: 69.6 us
  Pallas kernels  65.4 us (94%)
  local copies, waits for them, and re-layouts  4.12 us (6%)
    pallas_call x1, Pallas kernels, local(): pl.pallas_call(functools.partial(cycle_kernel, n_slab, n_mem), out_shape=...  65.4 us
    reshape x1, local copies, waits for them, and re-layouts, local(): swapped = states.reshape(kd // 8, 8, rows, lon).transpose(0, 2, 1, 3)  1.9 us
    transpose x1, local copies, waits for them, and re-layouts, local(): return out.transpose(1, 0, 2)  1.58 us

profile of v3, /device:TPU:0, one launch (start us, length us, event | category | flops | bytes accessed | tf_op | source)
XLA Modules:
  0.0 69.6 jit_solution(15592601621231600292)
XLA Ops:
  0.0 0.0 copy-start
  0.0 0.0 copy-start.1
  0.0 0.0 copy-start.4
  0.0 0.0 copy-start.5
  0.0 0.0 copy-start.6
  0.0 1.9 %copy.13 = f32[4,8,8,1024]{3,1,2,0:T(8,128)S(1)} copy(f32[4,8,8,1024]{3,2,1,0:T(8,128)} %bitcast.13) | data formatting | bytes 2097152 | tf_op jit(solution)/shard_map/reshape | solution.py:473
  1.9 0.0 copy-start.2
  1.9 0.0 copy-start.3
  1.9 0.0 copy-done
  2.0 0.0 copy-done.1
  2.0 0.0 copy-done.4
  2.0 0.0 copy-done.5
  2.0 0.0 copy-done.6
  2.0 0.6 copy-done.2
  2.6 0.0 copy-done.3
  2.6 65.4 %cycle.1 = f32[8,32,1024]{2,1,0:T(8,128)S(1)} custom-call(f32[4,8,8,1024]{3,2,1,0:T(8,128)S(1)} %bitcast.9, s32[8,1024]{1,0:T(8,128)S(1)} %copy-done, s32[8,1024]{1,0:T(8,128)S(1)} %copy-done.1, f32[8]{0:T(128)S(1)} %copy-done.3, f32[2,8]{1,0:T(2,128)S(1)} %copy-done.2, s32[1,128]{1,0:T(1,128)S(1)} %bitcast.10, f32[1,128]{1,0:T(1,128)S(1)} %bitcast.11, ...), custom_call_target="tpu_custom_call" | custom-call | tf_op jit(solution)/shard_map/cycle/pallas_call | solution.py:478
  68.0 1.6 %copy.11 = f32[32,8,1024]{2,1,0:T(8,128)} copy(f32[32,8,1024]{2,0,1:T(8,128)S(1)} %bitcast.8) | data formatting | bytes 2097152 | tf_op jit(solution)/shard_map/transpose | solution.py:509
Async XLA Ops:
  0.0 1.9 %copy-start = (s32[8,1024]{1,0:T(8,128)S(1)}, s32[8,1024]{1,0:T(8,128)}, u32[]{:S(2)}) copy-start(s32[8,1024]{1,0:T(8,128)} %classes_in.1) | copy-start | bytes 98308
  0.0 2.0 %copy-start.1 = (s32[8,1024]{1,0:T(8,128)S(1)}, s32[8,1024]{1,0:T(8,128)}, u32[]{:S(2)}) copy-start(s32[8,1024]{1,0:T(8,128)} %mask_in.1) | copy-start | bytes 98308
  0.0 2.0 %copy-start.4 = (s32[128]{0:T(128)S(1)}, s32[128]{0:T(128)}, u32[]{:S(2)}) copy-start(s32[128]{0:T(128)} %param.13) | copy-start | bytes 1540
  0.0 2.0 %copy-start.5 = (f32[128]{0:T(128)S(1)}, f32[128]{0:T(128)}, u32[]{:S(2)}) copy-start(f32[128]{0:T(128)} %param.14) | copy-start | bytes 1540
  0.0 2.0 %copy-start.6 = (f32[128]{0:T(128)S(1)}, f32[128]{0:T(128)}, u32[]{:S(2)}) copy-start(f32[128]{0:T(128)} %param.15) | copy-start | bytes 1540
  1.9 0.7 copy-start.2
  1.9 0.7 copy-start.3

commit v4 on v3

--- a/solution.py
+++ b/solution.py
@@ -42,7 +42,7 @@
     n_slab, n_mem,
     states, classes_in, mask_in, kappa, flow, obs_index, obs_values, obs_var,
     out,
-    buf, coef, geos, fore, mixed, gpart, grecv, gsum, precv, gfull, turned,
+    buf, coef, geos, fore, mixed, gpart, grecv, gsum, precv, gfull, turned, ready,
     geo_send, geo_recv, y_send, y_recv, d_send, r_send, z_recv, keep_sem,
     a_send, a_recv, s_send, s_recv, p_send, p_recv, g_send, g_recv, b_send, b_recv,
 ):
@@ -363,6 +363,8 @@
     for k in range(1, n_pair):
         p_copy(k).start()
     precv[q] = total
+    for row in range(rows):
+        ready[row] = right_parts(fore[0, row])
     for k in range(1, n_pair):
         p_wait(k).wait_recv()
     total = precv[0]
@@ -430,7 +432,7 @@
                     a_wait(j, c, *peer(k)).wait_recv()
         for h in range(CHUNKS):
             for row in range(depth * h, depth * h + depth):
-                result = product(weights, right_parts(fore[j, row]))
+                result = product(weights, ready[row] if j == 0 else right_parts(fore[j, row]))
                 mixed[j, row] = result[kd:]
                 out[row, :, pl.ds(start_at(m, j), span)] = result[:kd]
             b_copy(j, h).start()
@@ -492,6 +494,7 @@
             pltpu.VMEM((n_pair, block, 2 * ens), f32),
             pltpu.VMEM((ens, 2 * ens), f32),
             pltpu.VMEM((ens, ens), f32),
+            pltpu.VMEM((rows, 3 * ens, span), jnp.bfloat16),
             dma((3, 2)), dma((4, 2)), dma((octs, SPLIT)), dma((octs, SPLIT)), dma((octs, SPLIT)), dma((octs, SPLIT)),
             dma((2, octs, SPLIT)), dma((octs,)),
             dma((n_line, n_group, octs)), dma((n_line, n_group, octs)),

time: 69.8 us -> 69.4 us (level)
  no operation moved by 1% of the time
where the time goes in v4:
time: 69.4 us; the launch traced here: 69.2 us
  Pallas kernels  65.1 us (94%)
  local copies, waits for them, and re-layouts  4.12 us (6%)
    pallas_call x1, Pallas kernels, local(): pl.pallas_call(functools.partial(cycle_kernel, n_slab, n_mem), out_shape=...  65.1 us
    reshape x1, local copies, waits for them, and re-layouts, local(): swapped = states.reshape(kd // 8, 8, rows, lon).transpose(0, 2, 1, 3)  1.9 us
    transpose x1, local copies, waits for them, and re-layouts, local(): return out.transpose(1, 0, 2)  1.58 us

profile of v4, /device:TPU:0, one launch (start us, length us, event | category | flops | bytes accessed | tf_op | source)
XLA Modules:
  0.0 69.2 jit_solution(420733533419847231)
XLA Ops:
  0.0 0.0 copy-start
  0.0 0.0 copy-start.1
  0.0 0.0 copy-start.4
  0.0 0.0 copy-start.5
  0.0 0.0 copy-start.6
  0.0 1.9 %copy.13 = f32[4,8,8,1024]{3,1,2,0:T(8,128)S(1)} copy(f32[4,8,8,1024]{3,2,1,0:T(8,128)} %bitcast.13) | data formatting | bytes 2097152 | tf_op jit(solution)/shard_map/reshape | solution.py:475
  1.9 0.0 copy-start.2
  1.9 0.0 copy-start.3
  1.9 0.0 copy-done
  2.0 0.0 copy-done.1
  2.0 0.0 copy-done.4
  2.0 0.0 copy-done.5
  2.0 0.0 copy-done.6
  2.0 0.6 copy-done.2
  2.6 0.0 copy-done.3
  2.6 65.1 %cycle.1 = f32[8,32,1024]{2,1,0:T(8,128)S(1)} custom-call(f32[4,8,8,1024]{3,2,1,0:T(8,128)S(1)} %bitcast.9, s32[8,1024]{1,0:T(8,128)S(1)} %copy-done, s32[8,1024]{1,0:T(8,128)S(1)} %copy-done.1, f32[8]{0:T(128)S(1)} %copy-done.3, f32[2,8]{1,0:T(2,128)S(1)} %copy-done.2, s32[1,128]{1,0:T(1,128)S(1)} %bitcast.10, f32[1,128]{1,0:T(1,128)S(1)} %bitcast.11, ...), custom_call_target="tpu_custom_call" | custom-call | tf_op jit(solution)/shard_map/cycle/pallas_call | solution.py:480
  67.7 1.6 %copy.11 = f32[32,8,1024]{2,1,0:T(8,128)} copy(f32[32,8,1024]{2,0,1:T(8,128)S(1)} %bitcast.8) | data formatting | bytes 2097152 | tf_op jit(solution)/shard_map/transpose | solution.py:512
Async XLA Ops:
  0.0 1.9 %copy-start = (s32[8,1024]{1,0:T(8,128)S(1)}, s32[8,1024]{1,0:T(8,128)}, u32[]{:S(2)}) copy-start(s32[8,1024]{1,0:T(8,128)} %classes_in.1) | copy-start | bytes 98308
  0.0 2.0 %copy-start.1 = (s32[8,1024]{1,0:T(8,128)S(1)}, s32[8,1024]{1,0:T(8,128)}, u32[]{:S(2)}) copy-start(s32[8,1024]{1,0:T(8,128)} %mask_in.1) | copy-start | bytes 98308
  0.0 2.0 %copy-start.4 = (s32[128]{0:T(128)S(1)}, s32[128]{0:T(128)}, u32[]{:S(2)}) copy-start(s32[128]{0:T(128)} %param.13) | copy-start | bytes 1540
  0.0 2.0 %copy-start.5 = (f32[128]{0:T(128)S(1)}, f32[128]{0:T(128)}, u32[]{:S(2)}) copy-start(f32[128]{0:T(128)} %param.14) | copy-start | bytes 1540
  0.0 2.0 %copy-start.6 = (f32[128]{0:T(128)S(1)}, f32[128]{0:T(128)}, u32[]{:S(2)}) copy-start(f32[128]{0:T(128)} %param.15) | copy-start | bytes 1540
  1.9 0.7 copy-start.2
  1.9 0.7 copy-start.3
